TPU v7x, 256 devices: a whole 4x4x8 slice. The times are simulated.
256 devices in a mesh: gx: 8 (over z), gy: 8 (over y, core), gz: 4 (over x).
Axes of the slice: x: 4, y: 4, z: 8, core: 2. Of those that a mesh axis runs over, the one named last changes fastest.
Arguments:
- x_block: float32 [16, 64, 32, 512], P(None, 'gx', 'gy', 'gz'), may hold values from -6 to 6
- p_block: float32 [16, 64, 32, 512], P(None, 'gx', 'gy', 'gz'), may hold values from -6 to 6
- voxel_class: int32 [64, 32, 512], P('gx', 'gy', 'gz'), may hold values from 0 to 7
- conductance: float32 [8], replicated, may hold values from 0.25 to 4
Outputs:
- x_next: float32 [16, 64, 32, 512], P(None, 'gx', 'gy', 'gz')
- p_next: float32 [16, 64, 32, 512], P(None, 'gx', 'gy', 'gz')
All inputs are finite; a program needn't handle non-finite values.
Results may differ from a plain program's by a relative error of at most 0.0003.
Values sent between devices are 32-bit elements; how exact they have to be, the bound alone decides.
No kernel may reach another device: no remote copies, remote signals or barrier semaphores. Data moves between devices by JAX's collectives and lax.ppermute only.
A program may use at most 64 MiB of HBM per device.

v0:
```python
import jax
import jax.numpy as jnp
from jax import lax
from jax.sharding import PartitionSpec as P

VECS = 16
CLASSES = 8
ITERS = 2
INNER = 4
jacobi_weight = 2.0 / 3.0
mass_shift = 0.05


def with_halo(array, sides, width):
    for axis, dim in sides:
        peers, length = (lax.axis_size(axis), array.shape[dim])
        up = [(i, (i + 1) % peers) for i in range(peers - 1)]
        down = [(j, i) for i, j in up]
        last = lax.slice_in_dim(array, length - width, length, axis=dim)
        leading = lax.slice_in_dim(array, 0, width, axis=dim)
        before = lax.ppermute(last, axis, up)
        after = lax.ppermute(leading, axis, down)
        array = jnp.concatenate([before, array, after], axis=dim)
    return array


def matmul_high(first_side, second_side):
    return jnp.dot(first_side, second_side, precision=lax.Precision.HIGHEST)


def harmonic(one_side, other_side):
    return 2.0 * one_side * other_side / (one_side + other_side)


def fine_edges(padded):
    edge_x = harmonic(padded[:-1, 1:-1, 1:-1], padded[1:, 1:-1, 1:-1])
    edge_y = harmonic(padded[1:-1, :-1, 1:-1], padded[1:-1, 1:, 1:-1])
    edge_z = harmonic(padded[1:-1, 1:-1, :-1], padded[1:-1, 1:-1, 1:])
    return (edge_x, edge_y, edge_z)


def pair_sum(values, axis_index):
    old_shape = values.shape
    new_shape = (
        old_shape[:axis_index] + (old_shape[axis_index] // 2, 2) + old_shape[axis_index + 1 :]
    )
    return jnp.sum(values.reshape(new_shape), axis=axis_index + 1)


def coarsen_edges(edges):
    edge_x, edge_y, edge_z = edges
    coarse_x = pair_sum(pair_sum(edge_x[0::2], 1), 2)
    coarse_y = pair_sum(pair_sum(edge_y[:, 0::2], 0), 2)
    coarse_z = pair_sum(pair_sum(edge_z[:, :, 0::2], 0), 1)
    return (coarse_x, coarse_y, coarse_z)


def diagonal_of(edges, shift_term):
    edge_x, edge_y, edge_z = edges
    return (
        shift_term
        + edge_x[:-1]
        + edge_x[1:]
        + edge_y[:, :-1]
        + edge_y[:, 1:]
        + edge_z[:, :, :-1]
        + edge_z[:, :, 1:]
    )


def apply_operator(padded, field, edges, diagonal):
    edge_x, edge_y, edge_z = edges
    beside = edge_x[1:] * padded[:, 2:, 1:-1, 1:-1] + edge_x[:-1] * padded[:, :-2, 1:-1, 1:-1]
    beside = (
        beside
        + edge_y[:, 1:] * padded[:, 1:-1, 2:, 1:-1]
        + edge_y[:, :-1] * padded[:, 1:-1, :-2, 1:-1]
    )
    beside = (
        beside
        + edge_z[:, :, 1:] * padded[:, 1:-1, 1:-1, 2:]
        + edge_z[:, :, :-1] * padded[:, 1:-1, 1:-1, :-2]
    )
    return diagonal * field - beside


def smooth(residual, level_data, rim_fn):
    edges, diagonal = level_data
    first = jacobi_weight * residual / diagonal
    return (
        first
        + jacobi_weight
        * (residual - apply_operator(rim_fn(first), first, edges, diagonal))
        / diagonal
    )


def restrict(field):
    return pair_sum(pair_sum(pair_sum(field, 1), 2), 3)


def prolong(field):
    channels, size_x, size_y, size_z = field.shape
    wide = jnp.broadcast_to(
        field[:, :, None, :, None, :, None], (channels, size_x, 2, size_y, 2, size_z, 2)
    )
    return wide.reshape(channels, 2 * size_x, 2 * size_y, 2 * size_z)


def precondition(residual, levels, rims):
    middle_res = restrict(residual)
    coarse_res = restrict(middle_res)
    fine_part = smooth(residual, levels[0], rims[0])
    middle_part = smooth(middle_res, levels[1], rims[1])
    coarse_part = smooth(coarse_res, levels[2], rims[2])
    return fine_part + prolong(middle_part + prolong(coarse_part))


def solve_small(gram, cross):
    factor = jnp.linalg.cholesky(gram)
    partial_solve = jax.scipy.linalg.solve_triangular(factor, cross, lower=True)
    return jax.scipy.linalg.solve_triangular(factor, partial_solve, lower=True, trans="T")


def ritz_step(gram_b, gram_a, num_vecs, inner_steps):
    inverse_root = 1.0 / jnp.sqrt(jnp.diagonal(gram_b))
    outer_scale = inverse_root[:, None] * inverse_root[None, :]
    sym_a = 0.5 * (gram_a + gram_a.T)
    normed_b = 0.5 * (gram_b + gram_b.T) * outer_scale
    normed_a = sym_a * outer_scale
    factor_b = jnp.linalg.cholesky(normed_b)
    factor_a = jnp.linalg.cholesky(normed_a)
    sub_basis = jnp.eye(normed_b.shape[0], num_vecs, dtype=jnp.float32)
    for inner_step in range(inner_steps):
        lifted = matmul_high(factor_b, sub_basis)
        solved = jax.scipy.linalg.solve_triangular(factor_a, lifted, lower=True)
        solved = jax.scipy.linalg.solve_triangular(factor_a, solved, lower=True, trans="T")
        mapped = matmul_high(factor_b.T, solved)
        small_factor = jnp.linalg.cholesky(matmul_high(mapped.T, mapped))
        sub_basis = jax.scipy.linalg.solve_triangular(small_factor, mapped.T, lower=True).T
    coefficients = inverse_root[:, None] * jax.scipy.linalg.solve_triangular(
        factor_b, sub_basis, lower=True, trans="T"
    )
    rayleigh = matmul_high(coefficients.T, matmul_high(sym_a, coefficients))
    return (coefficients, rayleigh)


def fine_rim(field):
    return with_halo(field, (("gx", 1), ("gy", 2), ("gz", 3)), 1)


def middle_rim(field):
    return with_halo(field, (("gx", 1), ("gy", 2), ("gz", 3)), 1)


def coarse_rim(field):
    return with_halo(field, (("gx", 1), ("gy", 2), ("gz", 3)), 1)


def on_device(x_block, p_block, voxel_class, conductance):
    device_cells = x_block.shape[1] * x_block.shape[2] * x_block.shape[3]
    all_cells = device_cells * lax.axis_size("gx") * lax.axis_size("gy") * lax.axis_size("gz")
    local_cond = jnp.zeros(voxel_class.shape, jnp.float32)
    for class_index in range(CLASSES):
        local_cond = local_cond + jnp.where(
            voxel_class == class_index, conductance[class_index], 0.0
        )
    padded_first = fine_rim(jnp.concatenate([local_cond[None], x_block], 0))
    cond_pad = padded_first[0]
    x_pad = padded_first[1:]
    p_pad = fine_rim(p_block)
    fine_edge = fine_edges(cond_pad)
    middle_edge = coarsen_edges(fine_edge)
    coarse_edge = coarsen_edges(middle_edge)
    levels = (
        (fine_edge, diagonal_of(fine_edge, mass_shift)),
        (middle_edge, diagonal_of(middle_edge, 8.0 * mass_shift)),
        (coarse_edge, diagonal_of(coarse_edge, 64.0 * mass_shift)),
    )
    rims = (fine_rim, middle_rim, coarse_rim)
    block_x, block_p = (x_block, p_block)
    applied_x = apply_operator(x_pad, block_x, levels[0][0], levels[0][1])
    applied_p = apply_operator(p_pad, block_p, levels[0][0], levels[0][1])
    for iteration in range(ITERS):
        flat_x = block_x.reshape(VECS, -1)
        flat_ax = applied_x.reshape(VECS, -1)
        gram_x, cross_x = lax.psum(
            (matmul_high(flat_x, flat_x.T), matmul_high(flat_x, flat_ax.T)), ("gx", "gy", "gz")
        )
        projected = solve_small(gram_x / all_cells, cross_x / all_cells)
        residual = applied_x - matmul_high(projected.T, flat_x).reshape(block_x.shape)
        block_w = precondition(residual, levels, rims)
        applied_w = apply_operator(fine_rim(block_w), block_w, levels[0][0], levels[0][1])
        search = jnp.concatenate([block_x, block_w, block_p], 0).reshape(3 * VECS, -1)
        applied = jnp.concatenate([applied_x, applied_w, applied_p], 0).reshape(3 * VECS, -1)
        gram_b, gram_a = lax.psum(
            (matmul_high(search, search.T), matmul_high(search, applied.T)), ("gx", "gy", "gz")
        )
        coefficients, rayleigh = ritz_step(gram_b / all_cells, gram_a / all_cells, VECS, INNER)
        tail = coefficients[VECS:]
        block_x = matmul_high(coefficients.T, search).reshape(x_block.shape)
        applied_x = matmul_high(coefficients.T, applied).reshape(x_block.shape)
        block_p = matmul_high(tail.T, search[VECS:]).reshape(x_block.shape)
        applied_p = matmul_high(tail.T, applied[VECS:]).reshape(x_block.shape)
    return (block_x, block_p)


def solution(mesh):
    in_specs = (P(None, "gx", "gy", "gz"), P(None, "gx", "gy", "gz"), P("gx", "gy", "gz"), P())
    out_specs = (P(None, "gx", "gy", "gz"), P(None, "gx", "gy", "gz"))
    return jax.shard_map(
        on_device, mesh=mesh, in_specs=in_specs, out_specs=out_specs, check_vma=False
    )
```

profile of v0, /device:TPU:1, one launch (start us, length us, event | category | flops | bytes accessed | tf_op | source)
XLA Modules:
  0.0 719.8 jit_solution(8951026829940790295)
XLA Ops:
  3.4 5.8 select_add_fusion
  10.5 5.0 collective-permute-start
  16.6 3.5 collective-permute-start.31
  25.6 4.2 collective-permute-start.32
  29.8 3.1 collective-permute-start.33
  33.0 1.9 collective-permute-start.3
  34.9 3.6 collective-permute-start.2
  41.3 3.1 collective-permute-start.4
  47.2 4.8 collective-permute-start.35
  56.6 81.7 %all-reduce.3 = (f32[16,16]{0,1:T(8,128)S(1)}, f32[16,16]{0,1:T(8,128)S(1)}) all-reduce(f32[16,16]{0,1:T(8,128)S(1)} %convolution_bitcast_fusion.8, f32[16,16]{0,1:T(8,128)S(1)} %convolution_bitcast_fusion.7), channel_id=1, replica_groups=mesh['gx'=8,'gy'=8,'gz'=4] {'gx','gy','gz'}, use_global_device_ids=true, to_apply=%region_0.1 | all-reduce | flops 512 | bytes 4096 | tf_op jit(solution)/shard_map/psum | solution.py:187
  147.7 4.0 collective-permute-start.13
  154.5 4.0 collective-permute-start.19
  158.6 2.1 fusion.56
  162.4 4.0 collective-permute-start.7
  166.5 4.3 collective-permute-start.20
  170.7 2.7 collective-permute-start.21
  174.7 2.2 collective-permute-start.23
  178.2 2.3 collective-permute-start.14
  180.5 4.2 collective-permute-start.15
  188.0 4.9 collective-permute-start.17
  193.7 1.9 collective-permute-start.8
  195.7 4.7 collective-permute-start.9
  204.1 4.4 collective-permute-start.11
  213.5 3.9 collective-permute-done.11
  217.4 4.9 collective-permute-done.10
  225.1 4.0 collective-permute-start.25
  230.3 2.3 collective-permute-start.26
  232.6 5.4 collective-permute-start.27
  240.6 2.2 collective-permute-start.29
  251.0 4.9 collective-permute-done.28
  258.1 80.3 %all-reduce.2 = (f32[48,48]{0,1:T(8,128)S(1)}, f32[48,48]{1,0:T(8,128)S(1)}) all-reduce(f32[48,48]{0,1:T(8,128)S(1)} %copy-done.55, f32[48,48]{1,0:T(8,128)S(1)} %convolution_bitcast_fusion.2), channel_id=1, replica_groups=mesh['gx'=8,'gy'=8,'gz'=4] {'gx','gy','gz'}, use_global_device_ids=true, to_apply=%region_24.28 | all-reduce | flops 4608 | bytes 36864 | tf_op jit(solution)/shard_map/psum | solution.py:196
  339.9 4.4 cholesky.247
  346.6 4.4 cholesky.258
  352.5 3.7 custom-call.60
  381.0 3.7 custom-call.62
  387.5 75.2 %all-reduce.1 = (f32[16,16]{0,1:T(8,128)S(1)}, f32[16,16]{0,1:T(8,128)S(1)}) all-reduce(f32[16,16]{0,1:T(8,128)S(1)} %fusion.318, f32[16,16]{0,1:T(8,128)S(1)} %fusion.319), channel_id=1, replica_groups=mesh['gx'=8,'gy'=8,'gz'=4] {'gx','gy','gz'}, use_global_device_ids=true, to_apply=%region_28.36 | all-reduce | flops 512 | bytes 4096 | tf_op jit(solution)/shard_map/psum | solution.py:187
  474.7 4.6 collective-permute-start.43
  481.3 4.0 collective-permute-start.49
  491.1 4.0 collective-permute-start.37
  495.1 4.3 collective-permute-start.50
  499.4 1.9 collective-permute-start.51
  503.2 2.0 collective-permute-start.53
  506.5 2.7 collective-permute-start.44
  509.2 3.2 collective-permute-start.45
  513.9 1.9 collective-permute-start.38
  515.8 3.6 collective-permute-start.39
  521.0 4.9 collective-permute-start.47
  526.0 2.6 collective-permute-done.46
  528.7 1.8 collective-permute-done.47
  533.3 4.6 collective-permute-start.41
  543.0 4.6 collective-permute-done.41
  547.6 4.6 collective-permute-done.40
  552.2 1.8 fusion.44
  555.6 4.0 collective-permute-start.55
  560.6 4.9 collective-permute-start.56
  565.5 2.5 collective-permute-start.57
  570.6 3.8 collective-permute-start.59
  577.9 6.6 collective-permute-done.59
  584.5 5.0 collective-permute-done.58
  592.7 77.7 %all-reduce = (f32[48,48]{1,0:T(8,128)S(1)}, f32[48,48]{1,0:T(8,128)S(1)}) all-reduce(f32[48,48]{1,0:T(8,128)S(1)} %convolution_bitcast_fusion.1, f32[48,48]{1,0:T(8,128)S(1)} %convolution_bitcast_fusion), channel_id=1, replica_groups=mesh['gx'=8,'gy'=8,'gz'=4] {'gx','gy','gz'}, use_global_device_ids=true, to_apply=%region_37.45 | all-reduce | flops 4608 | bytes 36864 | tf_op jit(solution)/shard_map/psum | solution.py:196
  671.9 4.4 cholesky.324
  678.5 4.4 cholesky.335
  684.3 3.7 custom-call.75
  712.6 3.7 custom-call.77
  (565 shorter events, 177.1 us)
Async XLA Ops:
  9.2 23.7 %collective-permute-start.1 = (f32[17,1,4,128]{3,0,2,1:T(8,128)S(1)}, f32[17,1,4,128]{3,0,2,1:T(8,128)S(1)}, u32[]{:S(2)}, u32[]{:S(2)}) collective-permute-start(f32[17,1,4,128]{3,0,2,1:T(8,128)S(1)} %get-tuple-element.60), channel_id=1, source_target_pairs={{32,0},{64,32},{96,64},{128,96},{160,128},{192,160},{224,192},{33,... | collective-permute-start | bytes 104456 | tf_op jit(solution)/shard_map/ppermute | solution.py:22
  10.5 22.4 %collective-permute-start = (f32[17,1,4,128]{3,0,2,1:T(8,128)S(1)}, f32[17,1,4,128]{3,0,2,1:T(8,128)S(1)}, u32[]{:S(2)}, u32[]{:S(2)}) collective-permute-start(f32[17,1,4,128]{3,0,2,1:T(8,128)S(1)} %get-tuple-element.59), channel_id=1, source_target_pairs={{0,32},{32,64},{64,96},{96,128},{128,160},{160,192},{192,224},{1,3... | collective-permute-start | bytes 104456 | tf_op jit(solution)/shard_map/ppermute | solution.py:21
  16.6 7.8 %collective-permute-start.31 = (f32[16,1,4,128]{3,0,2,1:T(8,128)S(1)}, f32[16,1,4,128]{3,0,2,1:T(8,128)S(1)}, u32[]{:S(2)}, u32[]{:S(2)}) collective-permute-start(f32[16,1,4,128]{3,0,2,1:T(8,128)S(1)} %get-tuple-element.72), channel_id=1, source_target_pairs={{0,32},{32,64},{64,96},{96,128},{128,160},{160,192},{192,224},{1,3... | collective-permute-start | bytes 98312 | tf_op jit(solution)/shard_map/ppermute | solution.py:21
  20.2 4.8 collective-permute-start.30
  25.6 12.9 %collective-permute-start.32 = (f32[16,10,1,128]{3,0,2,1:T(8,128)S(1)}, f32[16,10,1,128]{3,0,2,1:T(8,128)S(1)}, u32[]{:S(2)}, u32[]{:S(2)}) collective-permute-start(f32[16,10,1,128]{3,0,2,1:T(8,128)S(1)} %get-tuple-element.56), channel_id=1, source_target_pairs={{4,0},{8,4},{12,8},{16,12},{20,16},{24,20},{28,24},{5,1},{9,5},{13... | collective-permute-start | bytes 245768 | tf_op jit(solution)/shard_map/ppermute | solution.py:22
  29.8 8.8 %collective-permute-start.33 = (f32[16,10,1,128]{3,0,2,1:T(8,128)S(1)}, f32[16,10,1,128]{3,0,2,1:T(8,128)S(1)}, u32[]{:S(2)}, u32[]{:S(2)}) collective-permute-start(f32[16,10,1,128]{3,0,2,1:T(8,128)S(1)} %get-tuple-element.55), channel_id=1, source_target_pairs={{0,4},{4,8},{8,12},{12,16},{16,20},{20,24},{24,28},{1,5},{5,9},{9,... | collective-permute-start | bytes 245768 | tf_op jit(solution)/shard_map/ppermute | solution.py:21
  33.0 6.2 collective-permute-start.3
  34.9 5.5 collective-permute-start.2
  41.3 12.0 %collective-permute-start.4 = (f32[17,10,6,1]{0,3,2,1:T(1,128)S(1)}, f32[17,10,6,1]{0,3,2,1:T(1,128)S(1)}, u32[]{:S(2)}, u32[]{:S(2)}) collective-permute-start(f32[17,10,6,1]{0,3,2,1:T(1,128)S(1)} %copy.640), channel_id=1, source_target_pairs={{0,1},{1,2},{2,3},{4,5},{5,6},{6,7},{8,9},{9,10},{10,11},{12,13},{... | collective-permute-start | bytes 12248 | tf_op jit(solution)/shard_map/ppermute | solution.py:21
  44.8 9.0 %collective-permute-start.5 = (f32[17,10,6,1]{0,3,2,1:T(1,128)S(1)}, f32[17,10,6,1]{0,3,2,1:T(1,128)S(1)}, u32[]{:S(2)}, u32[]{:S(2)}) collective-permute-start(f32[17,10,6,1]{0,3,2,1:T(1,128)S(1)} %copy.641), channel_id=1, source_target_pairs={{1,0},{2,1},{3,2},{5,4},{6,5},{7,6},{9,8},{10,9},{11,10},{13,12},{... | collective-permute-start | bytes 12248 | tf_op jit(solution)/shard_map/ppermute | solution.py:22
  47.2 107.3 %collective-permute-start.35 = (f32[16,10,6,1]{3,0,2,1:T(8,128)}, f32[16,10,6,1]{3,0,2,1:T(8,128)}, u32[]{:S(2)}, u32[]{:S(2)}) collective-permute-start(f32[16,10,6,1]{3,0,2,1:T(8,128)} %get-tuple-element.44), channel_id=1, source_target_pairs={{0,1},{1,2},{2,3},{4,5},{5,6},{6,7},{8,9},{9,10},{10,11},{12,13},{... | collective-permute-start | bytes 11528 | tf_op jit(solution)/shard_map/ppermute | solution.py:21
  52.0 106.5 %collective-permute-start.34 = (f32[16,10,6,1]{3,0,2,1:T(8,128)}, f32[16,10,6,1]{3,0,2,1:T(8,128)}, u32[]{:S(2)}, u32[]{:S(2)}) collective-permute-start(f32[16,10,6,1]{3,0,2,1:T(8,128)} %get-tuple-element.43), channel_id=1, source_target_pairs={{1,0},{2,1},{3,2},{5,4},{6,5},{7,6},{9,8},{10,9},{11,10},{13,12},{... | collective-permute-start | bytes 11528 | tf_op jit(solution)/shard_map/ppermute | solution.py:22
  55.5 155.1 %copy-start.40 = (f32[4,2,64]{2,1,0:T(2,128)}, f32[4,2,64]{2,1,0:T(2,128)S(1)}, u32[]{:S(2)}) copy-start(f32[4,2,64]{2,1,0:T(2,128)S(1)} %get-tuple-element.116) | copy-start | bytes 6148
  55.5 155.1 %copy-start.42 = (f32[4,2,64]{2,1,0:T(2,128)}, f32[4,2,64]{2,1,0:T(2,128)S(1)}, u32[]{:S(2)}) copy-start(f32[4,2,64]{2,1,0:T(2,128)S(1)} %get-tuple-element.117) | copy-start | bytes 6148
  146.4 24.3 %collective-permute-start.12 = (f32[16,1,2,64]{0,3,2,1:T(8,128)}, f32[16,1,2,64]{0,3,2,1:T(8,128)S(1)}, u32[]{:S(2)}, u32[]{:S(2)}) collective-permute-start(f32[16,1,2,64]{0,3,2,1:T(8,128)} %get-tuple-element.78), channel_id=1, source_target_pairs={{32,0},{64,32},{96,64},{128,96},{160,128},{192,160},{224,192},{33,... | collective-permute-start | bytes 24584 | tf_op jit(solution)/shard_map/ppermute | solution.py:22
  147.7 25.8 %collective-permute-start.13 = (f32[16,1,2,64]{0,3,2,1:T(8,128)}, f32[16,1,2,64]{0,3,2,1:T(8,128)S(1)}, u32[]{:S(2)}, u32[]{:S(2)}) collective-permute-start(f32[16,1,2,64]{0,3,2,1:T(8,128)} %get-tuple-element.77), channel_id=1, source_target_pairs={{0,32},{32,64},{64,96},{96,128},{128,160},{160,192},{192,224},{1,3... | collective-permute-start | bytes 24584 | tf_op jit(solution)/shard_map/ppermute | solution.py:21
  153.2 9.2 %collective-permute-start.18 = (f32[16,1,1,32]{0,3,1,2:T(8,128)S(1)}, f32[16,1,1,32]{0,3,1,2:T(8,128)S(1)}, u32[]{:S(2)}, u32[]{:S(2)}) collective-permute-start(f32[16,1,1,32]{0,3,1,2:T(8,128)S(1)} %get-tuple-element.106), channel_id=1, source_target_pairs={{32,0},{64,32},{96,64},{128,96},{160,128},{192,160},{224,192},{33,... | collective-permute-start | bytes 6152 | tf_op jit(solution)/shard_map/ppermute | solution.py:22
  154.5 11.9 %collective-permute-start.19 = (f32[16,1,1,32]{0,3,1,2:T(8,128)S(1)}, f32[16,1,1,32]{0,3,1,2:T(8,128)S(1)}, u32[]{:S(2)}, u32[]{:S(2)}) collective-permute-start(f32[16,1,1,32]{0,3,1,2:T(8,128)S(1)} %get-tuple-element.105), channel_id=1, source_target_pairs={{0,32},{32,64},{64,96},{96,128},{128,160},{160,192},{192,224},{1,3... | collective-permute-start | bytes 6152 | tf_op jit(solution)/shard_map/ppermute | solution.py:21
  160.9 49.8 %copy-start.44 = (f32[4,2,64]{2,1,0:T(2,128)}, f32[4,2,64]{2,1,0:T(2,128)S(1)}, u32[]{:S(2)}) copy-start(f32[4,2,64]{2,1,0:T(2,128)S(1)} %copy.668) | copy-start | bytes 6148
  161.1 31.8 %collective-permute-start.6 = (f32[16,1,4,128]{3,0,2,1:T(8,128)S(1)}, f32[16,1,4,128]{3,0,2,1:T(8,128)S(1)}, u32[]{:S(2)}, u32[]{:S(2)}) collective-permute-start(f32[16,1,4,128]{3,0,2,1:T(8,128)S(1)} %get-tuple-element.74), channel_id=1, source_target_pairs={{32,0},{64,32},{96,64},{128,96},{160,128},{192,160},{224,192},{33,... | collective-permute-start | bytes 98312 | tf_op jit(solution)/shard_map/ppermute | solution.py:22
  162.4 30.5 %collective-permute-start.7 = (f32[16,1,4,128]{3,0,2,1:T(8,128)S(1)}, f32[16,1,4,128]{3,0,2,1:T(8,128)S(1)}, u32[]{:S(2)}, u32[]{:S(2)}) collective-permute-start(f32[16,1,4,128]{3,0,2,1:T(8,128)S(1)} %get-tuple-element.73), channel_id=1, source_target_pairs={{0,32},{32,64},{64,96},{96,128},{128,160},{160,192},{192,224},{1,3... | collective-permute-start | bytes 98312 | tf_op jit(solution)/shard_map/ppermute | solution.py:21
  166.5 7.1 collective-permute-start.20
  170.7 4.0 collective-permute-start.21
  174.7 5.7 collective-permute-start.23
  176.9 7.8 %collective-permute-start.22 = (f32[16,4,3,1]{0,3,1,2:T(1,128)S(1)}, f32[16,4,3,1]{0,3,1,2:T(1,128)S(1)}, u32[]{:S(2)}, u32[]{:S(2)}) collective-permute-start(f32[16,4,3,1]{0,3,1,2:T(1,128)S(1)} %get-tuple-element.85), channel_id=1, source_target_pairs={{1,0},{2,1},{3,2},{5,4},{6,5},{7,6},{9,8},{10,9},{11,10},{13,12},{... | collective-permute-start | bytes 2312 | tf_op jit(solution)/shard_map/ppermute | solution.py:22
  178.2 7.3 %collective-permute-start.14 = (f32[16,6,1,64]{3,0,2,1:T(8,128)S(1)}, f32[16,6,1,64]{3,0,2,1:T(8,128)S(1)}, u32[]{:S(2)}, u32[]{:S(2)}) collective-permute-start(f32[16,6,1,64]{3,0,2,1:T(8,128)S(1)} %get-tuple-element.100), channel_id=1, source_target_pairs={{4,0},{8,4},{12,8},{16,12},{20,16},{24,20},{28,24},{5,1},{9,5},{13... | collective-permute-start | bytes 73736 | tf_op jit(solution)/shard_map/ppermute | solution.py:22
  180.5 5.4 collective-permute-start.15
  186.7 13.7 %collective-permute-start.16 = (f32[16,6,4,1]{3,0,2,1:T(8,128)}, f32[16,6,4,1]{3,0,2,1:T(8,128)S(1)}, u32[]{:S(2)}, u32[]{:S(2)}) collective-permute-start(f32[16,6,4,1]{3,0,2,1:T(8,128)} %get-tuple-element.89), channel_id=1, source_target_pairs={{1,0},{2,1},{3,2},{5,4},{6,5},{7,6},{9,8},{10,9},{11,10},{13,12},{... | collective-permute-start | bytes 4616 | tf_op jit(solution)/shard_map/ppermute | solution.py:22
  188.0 12.4 %collective-permute-start.17 = (f32[16,6,4,1]{3,0,2,1:T(8,128)}, f32[16,6,4,1]{3,0,2,1:T(8,128)S(1)}, u32[]{:S(2)}, u32[]{:S(2)}) collective-permute-start(f32[16,6,4,1]{3,0,2,1:T(8,128)} %get-tuple-element.90), channel_id=1, source_target_pairs={{0,1},{1,2},{2,3},{4,5},{5,6},{6,7},{8,9},{9,10},{10,11},{12,13},{... | collective-permute-start | bytes 4616 | tf_op jit(solution)/shard_map/ppermute | solution.py:21
  193.7 7.2 %collective-permute-start.8 = (f32[16,10,1,128]{3,0,2,1:T(8,128)}, f32[16,10,1,128]{3,0,2,1:T(8,128)S(1)}, u32[]{:S(2)}, u32[]{:S(2)}) collective-permute-start(f32[16,10,1,128]{3,0,2,1:T(8,128)} %get-tuple-element.58), channel_id=1, source_target_pairs={{4,0},{8,4},{12,8},{16,12},{20,16},{24,20},{28,24},{5,1},{9,5},{13... | collective-permute-start | bytes 245768 | tf_op jit(solution)/shard_map/ppermute | solution.py:22
  195.7 6.3 collective-permute-start.9
  204.1 13.3 %collective-permute-start.11 = (f32[16,10,6,1]{3,0,2,1:T(8,128)}, f32[16,10,6,1]{3,0,2,1:T(8,128)}, u32[]{:S(2)}, u32[]{:S(2)}) collective-permute-start(f32[16,10,6,1]{3,0,2,1:T(8,128)} %get-tuple-element.46), channel_id=1, source_target_pairs={{0,1},{1,2},{2,3},{4,5},{5,6},{6,7},{8,9},{9,10},{10,11},{12,13},{... | collective-permute-start | bytes 11528 | tf_op jit(solution)/shard_map/ppermute | solution.py:21
  208.5 13.7 %collective-permute-start.10 = (f32[16,10,6,1]{3,0,2,1:T(8,128)}, f32[16,10,6,1]{3,0,2,1:T(8,128)}, u32[]{:S(2)}, u32[]{:S(2)}) collective-permute-start(f32[16,10,6,1]{3,0,2,1:T(8,128)} %get-tuple-element.45), channel_id=1, source_target_pairs={{1,0},{2,1},{3,2},{5,4},{6,5},{7,6},{9,8},{10,9},{11,10},{13,12},{... | collective-permute-start | bytes 11528 | tf_op jit(solution)/shard_map/ppermute | solution.py:22
  223.8 5.4 collective-permute-start.24
  225.1 5.2 collective-permute-start.25
  230.3 7.9 %collective-permute-start.26 = (f32[16,10,1,128]{3,0,2,1:T(8,128)S(1)}, f32[16,10,1,128]{3,0,2,1:T(8,128)S(1)}, u32[]{:S(2)}, u32[]{:S(2)}) collective-permute-start(f32[16,10,1,128]{3,0,2,1:T(8,128)S(1)} %get-tuple-element.54), channel_id=1, source_target_pairs={{4,0},{8,4},{12,8},{16,12},{20,16},{24,20},{28,24},{5,1},{9,5},{13... | collective-permute-start | bytes 245768 | tf_op jit(solution)/shard_map/ppermute | solution.py:22
  232.6 6.9 collective-permute-start.27
  240.6 10.4 %collective-permute-start.29 = (f32[16,10,6,1]{3,0,2,1:T(8,128)}, f32[16,10,6,1]{3,0,2,1:T(8,128)}, u32[]{:S(2)}, u32[]{:S(2)}) collective-permute-start(f32[16,10,6,1]{3,0,2,1:T(8,128)} %get-tuple-element.42), channel_id=1, source_target_pairs={{0,1},{1,2},{2,3},{4,5},{5,6},{6,7},{8,9},{9,10},{10,11},{12,13},{... | collective-permute-start | bytes 11528 | tf_op jit(solution)/shard_map/ppermute | solution.py:21
  242.7 13.2 %collective-permute-start.28 = (f32[16,10,6,1]{3,0,2,1:T(8,128)}, f32[16,10,6,1]{3,0,2,1:T(8,128)}, u32[]{:S(2)}, u32[]{:S(2)}) collective-permute-start(f32[16,10,6,1]{3,0,2,1:T(8,128)} %get-tuple-element.41), channel_id=1, source_target_pairs={{1,0},{2,1},{3,2},{5,4},{6,5},{7,6},{9,8},{10,9},{11,10},{13,12},{... | collective-permute-start | bytes 11528 | tf_op jit(solution)/shard_map/ppermute | solution.py:22
  257.3 89.2 %copy-start.5 = (f32[16,8,4,128]{3,0,2,1:T(8,128)}, f32[16,8,4,128]{3,0,2,1:T(8,128)S(1)}, u32[]{:S(2)}) copy-start(f32[16,8,4,128]{3,0,2,1:T(8,128)S(1)} %fusion.68) | copy-start | bytes 786436
  473.4 26.0 %collective-permute-start.42 = (f32[16,1,2,64]{0,3,2,1:T(8,128)}, f32[16,1,2,64]{0,3,2,1:T(8,128)}, u32[]{:S(2)}, u32[]{:S(2)}) collective-permute-start(f32[16,1,2,64]{0,3,2,1:T(8,128)} %get-tuple-element.68), channel_id=1, source_target_pairs={{32,0},{64,32},{96,64},{128,96},{160,128},{192,160},{224,192},{33,... | collective-permute-start | bytes 24584 | tf_op jit(solution)/shard_map/ppermute | solution.py:22
  474.7 27.5 %collective-permute-start.43 = (f32[16,1,2,64]{0,3,2,1:T(8,128)}, f32[16,1,2,64]{0,3,2,1:T(8,128)}, u32[]{:S(2)}, u32[]{:S(2)}) collective-permute-start(f32[16,1,2,64]{0,3,2,1:T(8,128)} %get-tuple-element.67), channel_id=1, source_target_pairs={{0,32},{32,64},{64,96},{96,128},{128,160},{160,192},{192,224},{1,3... | collective-permute-start | bytes 24584 | tf_op jit(solution)/shard_map/ppermute | solution.py:21
  480.0 11.1 %collective-permute-start.48 = (f32[16,1,1,32]{0,3,1,2:T(8,128)S(1)}, f32[16,1,1,32]{0,3,1,2:T(8,128)S(1)}, u32[]{:S(2)}, u32[]{:S(2)}) collective-permute-start(f32[16,1,1,32]{0,3,1,2:T(8,128)S(1)} %get-tuple-element.104), channel_id=1, source_target_pairs={{32,0},{64,32},{96,64},{128,96},{160,128},{192,160},{224,192},{33,... | collective-permute-start | bytes 6152 | tf_op jit(solution)/shard_map/ppermute | solution.py:22
  481.3 13.8 %collective-permute-start.49 = (f32[16,1,1,32]{0,3,1,2:T(8,128)S(1)}, f32[16,1,1,32]{0,3,1,2:T(8,128)S(1)}, u32[]{:S(2)}, u32[]{:S(2)}) collective-permute-start(f32[16,1,1,32]{0,3,1,2:T(8,128)S(1)} %get-tuple-element.103), channel_id=1, source_target_pairs={{0,32},{32,64},{64,96},{96,128},{128,160},{160,192},{192,224},{1,3... | collective-permute-start | bytes 6152 | tf_op jit(solution)/shard_map/ppermute | solution.py:21
  488.9 24.4 %collective-permute-start.36 = (f32[16,1,4,128]{3,0,2,1:T(8,128)S(1)}, f32[16,1,4,128]{3,0,2,1:T(8,128)S(1)}, u32[]{:S(2)}, u32[]{:S(2)}) collective-permute-start(f32[16,1,4,128]{3,0,2,1:T(8,128)S(1)} %get-tuple-element.66), channel_id=1, source_target_pairs={{32,0},{64,32},{96,64},{128,96},{160,128},{192,160},{224,192},{33,... | collective-permute-start | bytes 98312 | tf_op jit(solution)/shard_map/ppermute | solution.py:22
  491.1 22.2 %collective-permute-start.37 = (f32[16,1,4,128]{3,0,2,1:T(8,128)S(1)}, f32[16,1,4,128]{3,0,2,1:T(8,128)S(1)}, u32[]{:S(2)}, u32[]{:S(2)}) collective-permute-start(f32[16,1,4,128]{3,0,2,1:T(8,128)S(1)} %get-tuple-element.65), channel_id=1, source_target_pairs={{0,32},{32,64},{64,96},{96,128},{128,160},{160,192},{192,224},{1,3... | collective-permute-start | bytes 98312 | tf_op jit(solution)/shard_map/ppermute | solution.py:21
  495.1 8.1 %collective-permute-start.50 = (f32[16,4,1,32]{0,3,1,2:T(8,128)S(1)}, f32[16,4,1,32]{0,3,1,2:T(8,128)S(1)}, u32[]{:S(2)}, u32[]{:S(2)}) collective-permute-start(f32[16,4,1,32]{0,3,1,2:T(8,128)S(1)} %pad_maximum_fusion.177), channel_id=1, source_target_pairs={{4,0},{8,4},{12,8},{16,12},{20,16},{24,20},{28,24},{5,1},{9,5},{13... | collective-permute-start | bytes 24584 | tf_op jit(solution)/shard_map/ppermute | solution.py:22
  499.4 3.8 collective-permute-start.51
  503.2 6.0 collective-permute-start.53
  505.2 7.3 %collective-permute-start.52 = (f32[16,4,3,1]{0,3,1,2:T(1,128)S(1)}, f32[16,4,3,1]{0,3,1,2:T(1,128)S(1)}, u32[]{:S(2)}, u32[]{:S(2)}) collective-permute-start(f32[16,4,3,1]{0,3,1,2:T(1,128)S(1)} %get-tuple-element.79), channel_id=1, source_target_pairs={{1,0},{2,1},{3,2},{5,4},{6,5},{7,6},{9,8},{10,9},{11,10},{13,12},{... | collective-permute-start | bytes 2312 | tf_op jit(solution)/shard_map/ppermute | solution.py:22
  506.5 13.0 %collective-permute-start.44 = (f32[16,6,1,64]{3,0,2,1:T(8,128)S(1)}, f32[16,6,1,64]{3,0,2,1:T(8,128)S(1)}, u32[]{:S(2)}, u32[]{:S(2)}) collective-permute-start(f32[16,6,1,64]{3,0,2,1:T(8,128)S(1)} %get-tuple-element.94), channel_id=1, source_target_pairs={{4,0},{8,4},{12,8},{16,12},{20,16},{24,20},{28,24},{5,1},{9,5},{13... | collective-permute-start | bytes 73736 | tf_op jit(solution)/shard_map/ppermute | solution.py:22
  509.2 10.3 %collective-permute-start.45 = (f32[16,6,1,64]{3,0,2,1:T(8,128)S(1)}, f32[16,6,1,64]{3,0,2,1:T(8,128)S(1)}, u32[]{:S(2)}, u32[]{:S(2)}) collective-permute-start(f32[16,6,1,64]{3,0,2,1:T(8,128)S(1)} %get-tuple-element.93), channel_id=1, source_target_pairs={{0,4},{4,8},{8,12},{12,16},{16,20},{20,24},{24,28},{1,5},{5,9},{9,... | collective-permute-start | bytes 73736 | tf_op jit(solution)/shard_map/ppermute | solution.py:21
  513.9 17.2 %collective-permute-start.38 = (f32[16,10,1,128]{3,0,2,1:T(8,128)}, f32[16,10,1,128]{3,0,2,1:T(8,128)}, u32[]{:S(2)}, u32[]{:S(2)}) collective-permute-start(f32[16,10,1,128]{3,0,2,1:T(8,128)} %get-tuple-element.52), channel_id=1, source_target_pairs={{4,0},{8,4},{12,8},{16,12},{20,16},{24,20},{28,24},{5,1},{9,5},{13... | collective-permute-start | bytes 245768 | tf_op jit(solution)/shard_map/ppermute | solution.py:22
  515.8 15.3 %collective-permute-start.39 = (f32[16,10,1,128]{3,0,2,1:T(8,128)}, f32[16,10,1,128]{3,0,2,1:T(8,128)}, u32[]{:S(2)}, u32[]{:S(2)}) collective-permute-start(f32[16,10,1,128]{3,0,2,1:T(8,128)} %get-tuple-element.51), channel_id=1, source_target_pairs={{0,4},{4,8},{8,12},{12,16},{16,20},{20,24},{24,28},{1,5},{5,9},{9,... | collective-permute-start | bytes 245768 | tf_op jit(solution)/shard_map/ppermute | solution.py:21
  519.7 9.0 %collective-permute-start.46 = (f32[16,6,4,1]{3,0,2,1:T(8,128)S(1)}, f32[16,6,4,1]{3,0,2,1:T(8,128)S(1)}, u32[]{:S(2)}, u32[]{:S(2)}) collective-permute-start(f32[16,6,4,1]{3,0,2,1:T(8,128)S(1)} %get-tuple-element.83), channel_id=1, source_target_pairs={{1,0},{2,1},{3,2},{5,4},{6,5},{7,6},{9,8},{10,9},{11,10},{13,12},{... | collective-permute-start | bytes 4616 | tf_op jit(solution)/shard_map/ppermute | solution.py:22
  521.0 9.5 %collective-permute-start.47 = (f32[16,6,4,1]{3,0,2,1:T(8,128)S(1)}, f32[16,6,4,1]{3,0,2,1:T(8,128)S(1)}, u32[]{:S(2)}, u32[]{:S(2)}) collective-permute-start(f32[16,6,4,1]{3,0,2,1:T(8,128)S(1)} %get-tuple-element.84), channel_id=1, source_target_pairs={{0,1},{1,2},{2,3},{4,5},{5,6},{6,7},{8,9},{9,10},{10,11},{12,13},{... | collective-permute-start | bytes 4616 | tf_op jit(solution)/shard_map/ppermute | solution.py:21
  533.3 14.4 %collective-permute-start.41 = (f32[16,10,6,1]{3,0,2,1:T(8,128)}, f32[16,10,6,1]{3,0,2,1:T(8,128)}, u32[]{:S(2)}, u32[]{:S(2)}) collective-permute-start(f32[16,10,6,1]{3,0,2,1:T(8,128)} %get-tuple-element.40), channel_id=1, source_target_pairs={{0,1},{1,2},{2,3},{4,5},{5,6},{6,7},{8,9},{9,10},{10,11},{12,13},{... | collective-permute-start | bytes 11528 | tf_op jit(solution)/shard_map/ppermute | solution.py:21
  537.9 14.3 %collective-permute-start.40 = (f32[16,10,6,1]{3,0,2,1:T(8,128)}, f32[16,10,6,1]{3,0,2,1:T(8,128)}, u32[]{:S(2)}, u32[]{:S(2)}) collective-permute-start(f32[16,10,6,1]{3,0,2,1:T(8,128)} %get-tuple-element.39), channel_id=1, source_target_pairs={{1,0},{2,1},{3,2},{5,4},{6,5},{7,6},{9,8},{10,9},{11,10},{13,12},{... | collective-permute-start | bytes 11528 | tf_op jit(solution)/shard_map/ppermute | solution.py:22
  554.3 5.4 collective-permute-start.54
  555.6 5.0 collective-permute-start.55
  560.6 7.5 %collective-permute-start.56 = (f32[16,10,1,128]{3,0,2,1:T(8,128)S(1)}, f32[16,10,1,128]{3,0,2,1:T(8,128)S(1)}, u32[]{:S(2)}, u32[]{:S(2)}) collective-permute-start(f32[16,10,1,128]{3,0,2,1:T(8,128)S(1)} %get-tuple-element.50), channel_id=1, source_target_pairs={{4,0},{8,4},{12,8},{16,12},{20,16},{24,20},{28,24},{5,1},{9,5},{13... | collective-permute-start | bytes 245768 | tf_op jit(solution)/shard_map/ppermute | solution.py:22
  565.5 3.9 collective-permute-start.57
  570.6 14.0 %collective-permute-start.59 = (f32[16,10,6,1]{3,0,2,1:T(8,128)}, f32[16,10,6,1]{3,0,2,1:T(8,128)}, u32[]{:S(2)}, u32[]{:S(2)}) collective-permute-start(f32[16,10,6,1]{3,0,2,1:T(8,128)} %get-tuple-element.38), channel_id=1, source_target_pairs={{0,1},{1,2},{2,3},{4,5},{5,6},{6,7},{8,9},{9,10},{10,11},{12,13},{... | collective-permute-start | bytes 11528 | tf_op jit(solution)/shard_map/ppermute | solution.py:21
  574.4 15.2 %collective-permute-start.58 = (f32[16,10,6,1]{3,0,2,1:T(8,128)}, f32[16,10,6,1]{3,0,2,1:T(8,128)}, u32[]{:S(2)}, u32[]{:S(2)}) collective-permute-start(f32[16,10,6,1]{3,0,2,1:T(8,128)} %get-tuple-element.37), channel_id=1, source_target_pairs={{1,0},{2,1},{3,2},{5,4},{6,5},{7,6},{9,8},{10,9},{11,10},{13,12},{... | collective-permute-start | bytes 11528 | tf_op jit(solution)/shard_map/ppermute | solution.py:22
  (64 other events, 1041.1 us)
where the time goes:
time: 731 us; the launch traced here: 720 us
  blocking collectives  315 us (43%)
  starting transfers between devices  169 us (23%)
  other arithmetic  106 us (15%)
  waiting for transfers between devices  49.4 us (7%)
  local copies, waits for them, and re-layouts  43.5 us (6%)
  matrix products  33 us (5%)
    psum x2, blocking collectives, on_device(): lax.psum((matmul_high(search, search.T), matmul_high(search, applied.T)),...  158 us
    psum x2, blocking collectives, on_device(): lax.psum((matmul_high(flat_x, flat_x.T), matmul_high(flat_x, flat_ax.T)),...  157 us
    ppermute x30, starting transfers between devices, with_halo(): before = lax.ppermute(last, axis, up)  113 us
    ppermute x30, starting transfers between devices, with_halo(): after = lax.ppermute(leading, axis, down)  56.3 us
    dot_general x40, matrix products, matmul_high(): return jnp.dot(first_side, second_side, precision=lax.Precision.HIGHEST)  27.9 us
    ppermute x30, waiting for transfers between devices, with_halo(): before = lax.ppermute(last, axis, up)  26.1 us
    ppermute x30, waiting for transfers between devices, with_halo(): after = lax.ppermute(leading, axis, down)  23.2 us
    another operation x24, other arithmetic, ritz_step(): small_factor = jnp.linalg.cholesky(matmul_high(mapped.T, mapped))  17.5 us
  transfers between devices with their start and end apart: 60, of which 22 were waited for; matrix products, arithmetic and copies ran while one was open for 7% of the time, Pallas kernels for 0%

commit v1 on v0

--- a/solution.py
+++ b/solution.py
@@ -194,7 +194,8 @@
         search = jnp.concatenate([block_x, block_w, block_p], 0).reshape(3 * VECS, -1)
         applied = jnp.concatenate([applied_x, applied_w, applied_p], 0).reshape(3 * VECS, -1)
         gram_b, gram_a = lax.psum(
-            (matmul_high(search, search.T), matmul_high(search, applied.T)), ("gx", "gy", "gz")
+            lax.psum((matmul_high(search, search.T), matmul_high(search, applied.T)), "gx"),
+            ("gy", "gz"),
         )
         coefficients, rayleigh = ritz_step(gram_b / all_cells, gram_a / all_cells, VECS, INNER)
         tail = coefficients[VECS:]

time: 731 us -> 883 us (1.21)
  blocking collectives: 315 us -> 462 us
    psum x0 -> x2, blocking collectives: none -> 251 us  [on_device(): lax.psum(lax.psum((matmul_high(search, search.T), matmul_high(search, app...]
    psum x2, blocking collectives: 158 us -> 51.9 us  [on_device(): lax.psum((matmul_high(search, search.T), matmul_high(search, applied.T)),...]
  transfers between devices with their start and end apart: 60 -> 60, of which waited for: 22 -> 22; matrix products, arithmetic and copies ran while one was open for 7% -> 5% of each run, Pallas kernels for 0% -> 0%
where the time goes in v1:
time: 883 us; the launch traced here: 868 us
  blocking collectives  462 us (52%)
  starting transfers between devices  171 us (19%)
  other arithmetic  106 us (12%)
  waiting for transfers between devices  49.9 us (6%)
  local copies, waits for them, and re-layouts  43.5 us (5%)
  matrix products  32.4 us (4%)
    psum x2, blocking collectives, on_device(): lax.psum(lax.psum((matmul_high(search, search.T), matmul_high(search, app...  251 us
    psum x2, blocking collectives, on_device(): lax.psum((matmul_high(flat_x, flat_x.T), matmul_high(flat_x, flat_ax.T)),...  159 us
    ppermute x30, starting transfers between devices, with_halo(): before = lax.ppermute(last, axis, up)  115 us
    ppermute x30, starting transfers between devices, with_halo(): after = lax.ppermute(leading, axis, down)  56.2 us
    psum x2, blocking collectives, on_device(): lax.psum((matmul_high(search, search.T), matmul_high(search, applied.T)),...  51.9 us
    dot_general x40, matrix products, matmul_high(): return jnp.dot(first_side, second_side, precision=lax.Precision.HIGHEST)  27.3 us
    ppermute x30, waiting for transfers between devices, with_halo(): before = lax.ppermute(last, axis, up)  26.7 us
    ppermute x30, waiting for transfers between devices, with_halo(): after = lax.ppermute(leading, axis, down)  23.2 us
  transfers between devices with their start and end apart: 60, of which 22 were waited for; matrix products, arithmetic and copies ran while one was open for 5% of the time, Pallas kernels for 0%

profile of v1, /device:TPU:1, one launch (start us, length us, event | category | flops | bytes accessed | tf_op | source)
XLA Modules:
  0.0 868.2 jit_solution(17461294971919931503)
XLA Ops:
  3.4 5.8 select_add_fusion
  10.5 5.0 collective-permute-start
  16.6 3.5 collective-permute-start.31
  25.6 4.2 collective-permute-start.32
  29.8 3.1 collective-permute-start.33
  33.0 1.9 collective-permute-start.3
  34.9 3.6 collective-permute-start.2
  41.3 3.1 collective-permute-start.4
  47.2 4.8 collective-permute-start.35
  56.6 81.7 %all-reduce.1 = (f32[16,16]{0,1:T(8,128)S(1)}, f32[16,16]{0,1:T(8,128)S(1)}) all-reduce(f32[16,16]{0,1:T(8,128)S(1)} %convolution_bitcast_fusion.8, f32[16,16]{0,1:T(8,128)S(1)} %convolution_bitcast_fusion.7), channel_id=1, replica_groups=mesh['gx'=8,'gy'=8,'gz'=4] {'gx','gy','gz'}, use_global_device_ids=true, to_apply=%region_0.1 | all-reduce | flops 512 | bytes 4096 | tf_op jit(solution)/shard_map/psum | solution.py:187
  147.7 4.0 collective-permute-start.13
  154.5 4.0 collective-permute-start.19
  158.6 2.1 fusion.56
  162.4 4.0 collective-permute-start.7
  166.5 4.3 collective-permute-start.20
  170.8 2.7 collective-permute-start.21
  174.8 2.2 collective-permute-start.23
  178.2 2.3 collective-permute-start.14
  180.5 4.2 collective-permute-start.15
  188.0 4.9 collective-permute-start.17
  193.8 1.9 collective-permute-start.8
  195.7 4.7 collective-permute-start.9
  204.1 4.4 collective-permute-start.11
  213.5 3.9 collective-permute-done.11
  217.4 4.9 collective-permute-done.10
  225.1 4.0 collective-permute-start.25
  230.3 2.3 collective-permute-start.26
  232.6 5.4 collective-permute-start.27
  240.6 2.1 collective-permute-start.29
  249.0 2.0 collective-permute-done.29
  251.0 4.9 collective-permute-done.28
  258.1 26.4 %all-reduce.5 = (f32[48,48]{0,1:T(8,128)S(1)}, f32[48,48]{1,0:T(8,128)S(1)}) all-reduce(f32[48,48]{0,1:T(8,128)S(1)} %convolution_bitcast_fusion.3, f32[48,48]{1,0:T(8,128)S(1)} %convolution_bitcast_fusion.2), channel_id=1, replica_groups=mesh['gx'=8,'gy'=8,'gz'=4] {'gx'}, use_global_device_ids=true, to_apply=%region_24.28 | all-reduce | flops 4608 | bytes 36864 | tf_op jit(solution)/shard_map/psum | solution.py:197
  284.5 124.8 %all-reduce.3 = (f32[48,48]{0,1:T(8,128)S(1)}, f32[48,48]{1,0:T(8,128)S(1)}) all-reduce(f32[48,48]{0,1:T(8,128)S(1)} %get-tuple-element.37, f32[48,48]{1,0:T(8,128)S(1)} %get-tuple-element.38), channel_id=1, replica_groups=mesh['gx'=8,'gy'=8,'gz'=4] {'gy','gz'}, use_global_device_ids=true, to_apply=%region_25.29 | all-reduce | flops 4608 | bytes 36864 | tf_op jit(solution)/shard_map/psum | solution.py:196
  410.7 4.4 cholesky.247
  417.4 4.4 cholesky.258
  423.3 3.7 custom-call.60
  451.9 3.7 custom-call.62
  458.3 77.0 %all-reduce = (f32[16,16]{0,1:T(8,128)S(1)}, f32[16,16]{0,1:T(8,128)S(1)}) all-reduce(f32[16,16]{0,1:T(8,128)S(1)} %fusion.318, f32[16,16]{0,1:T(8,128)S(1)} %fusion.319), channel_id=1, replica_groups=mesh['gx'=8,'gy'=8,'gz'=4] {'gx','gy','gz'}, use_global_device_ids=true, to_apply=%region_30.38 | all-reduce | flops 512 | bytes 4096 | tf_op jit(solution)/shard_map/psum | solution.py:187
  547.4 5.0 collective-permute-start.43
  554.4 4.0 collective-permute-start.49
  564.2 4.0 collective-permute-start.37
  568.2 4.3 collective-permute-start.50
  572.4 3.1 collective-permute-start.51
  577.4 2.1 collective-permute-start.53
  580.8 2.7 collective-permute-start.44
  583.5 3.2 collective-permute-start.45
  590.2 3.6 collective-permute-start.39
  595.3 4.9 collective-permute-start.47
  600.4 2.6 collective-permute-done.46
  607.6 4.6 collective-permute-start.41
  617.3 4.6 collective-permute-done.41
  622.0 4.6 collective-permute-done.40
  629.9 4.0 collective-permute-start.55
  635.0 4.7 collective-permute-start.56
  639.7 2.4 collective-permute-start.57
  644.7 3.9 collective-permute-start.59
  652.1 6.6 collective-permute-done.59
  658.7 5.0 collective-permute-done.58
  666.9 25.6 %all-reduce.4 = (f32[48,48]{1,0:T(8,128)S(1)}, f32[48,48]{1,0:T(8,128)S(1)}) all-reduce(f32[48,48]{1,0:T(8,128)S(1)} %convolution_bitcast_fusion.1, f32[48,48]{1,0:T(8,128)S(1)} %convolution_bitcast_fusion), channel_id=1, replica_groups=mesh['gx'=8,'gy'=8,'gz'=4] {'gx'}, use_global_device_ids=true, to_apply=%region_39.47 | all-reduce | flops 4608 | bytes 36864 | tf_op jit(solution)/shard_map/psum | solution.py:197
  692.5 126.4 %all-reduce.2 = (f32[48,48]{1,0:T(8,128)S(1)}, f32[48,48]{1,0:T(8,128)S(1)}) all-reduce(f32[48,48]{1,0:T(8,128)S(1)} %get-tuple-element.35, f32[48,48]{1,0:T(8,128)S(1)} %get-tuple-element.36), channel_id=1, replica_groups=mesh['gx'=8,'gy'=8,'gz'=4] {'gy','gz'}, use_global_device_ids=true, to_apply=%region_40.48 | all-reduce | flops 4608 | bytes 36864 | tf_op jit(solution)/shard_map/psum | solution.py:196
  820.3 4.4 cholesky.324
  826.9 4.4 cholesky.335
  832.6 3.7 custom-call.75
  861.0 3.7 custom-call.77
  (565 shorter events, 180.6 us)
Async XLA Ops:
  9.2 23.7 %collective-permute-start.1 = (f32[17,1,4,128]{3,0,2,1:T(8,128)S(1)}, f32[17,1,4,128]{3,0,2,1:T(8,128)S(1)}, u32[]{:S(2)}, u32[]{:S(2)}) collective-permute-start(f32[17,1,4,128]{3,0,2,1:T(8,128)S(1)} %get-tuple-element.64), channel_id=1, source_target_pairs={{32,0},{64,32},{96,64},{128,96},{160,128},{192,160},{224,192},{33,... | collective-permute-start | bytes 104456 | tf_op jit(solution)/shard_map/ppermute | solution.py:22
  10.5 22.4 %collective-permute-start = (f32[17,1,4,128]{3,0,2,1:T(8,128)S(1)}, f32[17,1,4,128]{3,0,2,1:T(8,128)S(1)}, u32[]{:S(2)}, u32[]{:S(2)}) collective-permute-start(f32[17,1,4,128]{3,0,2,1:T(8,128)S(1)} %get-tuple-element.63), channel_id=1, source_target_pairs={{0,32},{32,64},{64,96},{96,128},{128,160},{160,192},{192,224},{1,3... | collective-permute-start | bytes 104456 | tf_op jit(solution)/shard_map/ppermute | solution.py:21
  16.6 7.8 collective-permute-start.31
  20.2 4.8 collective-permute-start.30
  25.6 12.9 %collective-permute-start.32 = (f32[16,10,1,128]{3,0,2,1:T(8,128)S(1)}, f32[16,10,1,128]{3,0,2,1:T(8,128)S(1)}, u32[]{:S(2)}, u32[]{:S(2)}) collective-permute-start(f32[16,10,1,128]{3,0,2,1:T(8,128)S(1)} %get-tuple-element.60), channel_id=1, source_target_pairs={{4,0},{8,4},{12,8},{16,12},{20,16},{24,20},{28,24},{5,1},{9,5},{13... | collective-permute-start | bytes 245768 | tf_op jit(solution)/shard_map/ppermute | solution.py:22
  29.8 8.8 %collective-permute-start.33 = (f32[16,10,1,128]{3,0,2,1:T(8,128)S(1)}, f32[16,10,1,128]{3,0,2,1:T(8,128)S(1)}, u32[]{:S(2)}, u32[]{:S(2)}) collective-permute-start(f32[16,10,1,128]{3,0,2,1:T(8,128)S(1)} %get-tuple-element.59), channel_id=1, source_target_pairs={{0,4},{4,8},{8,12},{12,16},{16,20},{20,24},{24,28},{1,5},{5,9},{9,... | collective-permute-start | bytes 245768 | tf_op jit(solution)/shard_map/ppermute | solution.py:21
  33.0 6.2 collective-permute-start.3
  34.9 5.5 collective-permute-start.2
  41.3 12.0 %collective-permute-start.4 = (f32[17,10,6,1]{0,3,2,1:T(1,128)S(1)}, f32[17,10,6,1]{0,3,2,1:T(1,128)S(1)}, u32[]{:S(2)}, u32[]{:S(2)}) collective-permute-start(f32[17,10,6,1]{0,3,2,1:T(1,128)S(1)} %copy.640), channel_id=1, source_target_pairs={{0,1},{1,2},{2,3},{4,5},{5,6},{6,7},{8,9},{9,10},{10,11},{12,13},{... | collective-permute-start | bytes 12248 | tf_op jit(solution)/shard_map/ppermute | solution.py:21
  44.8 9.0 %collective-permute-start.5 = (f32[17,10,6,1]{0,3,2,1:T(1,128)S(1)}, f32[17,10,6,1]{0,3,2,1:T(1,128)S(1)}, u32[]{:S(2)}, u32[]{:S(2)}) collective-permute-start(f32[17,10,6,1]{0,3,2,1:T(1,128)S(1)} %copy.641), channel_id=1, source_target_pairs={{1,0},{2,1},{3,2},{5,4},{6,5},{7,6},{9,8},{10,9},{11,10},{13,12},{... | collective-permute-start | bytes 12248 | tf_op jit(solution)/shard_map/ppermute | solution.py:22
  47.2 107.3 %collective-permute-start.35 = (f32[16,10,6,1]{3,0,2,1:T(8,128)}, f32[16,10,6,1]{3,0,2,1:T(8,128)}, u32[]{:S(2)}, u32[]{:S(2)}) collective-permute-start(f32[16,10,6,1]{3,0,2,1:T(8,128)} %get-tuple-element.48), channel_id=1, source_target_pairs={{0,1},{1,2},{2,3},{4,5},{5,6},{6,7},{8,9},{9,10},{10,11},{12,13},{... | collective-permute-start | bytes 11528 | tf_op jit(solution)/shard_map/ppermute | solution.py:21
  52.0 106.5 %collective-permute-start.34 = (f32[16,10,6,1]{3,0,2,1:T(8,128)}, f32[16,10,6,1]{3,0,2,1:T(8,128)}, u32[]{:S(2)}, u32[]{:S(2)}) collective-permute-start(f32[16,10,6,1]{3,0,2,1:T(8,128)} %get-tuple-element.47), channel_id=1, source_target_pairs={{1,0},{2,1},{3,2},{5,4},{6,5},{7,6},{9,8},{10,9},{11,10},{13,12},{... | collective-permute-start | bytes 11528 | tf_op jit(solution)/shard_map/ppermute | solution.py:22
  55.5 155.1 %copy-start.40 = (f32[4,2,64]{2,1,0:T(2,128)}, f32[4,2,64]{2,1,0:T(2,128)S(1)}, u32[]{:S(2)}) copy-start(f32[4,2,64]{2,1,0:T(2,128)S(1)} %get-tuple-element.120) | copy-start | bytes 6148
  55.5 155.1 %copy-start.42 = (f32[4,2,64]{2,1,0:T(2,128)}, f32[4,2,64]{2,1,0:T(2,128)S(1)}, u32[]{:S(2)}) copy-start(f32[4,2,64]{2,1,0:T(2,128)S(1)} %get-tuple-element.121) | copy-start | bytes 6148
  146.4 24.3 %collective-permute-start.12 = (f32[16,1,2,64]{0,3,2,1:T(8,128)}, f32[16,1,2,64]{0,3,2,1:T(8,128)S(1)}, u32[]{:S(2)}, u32[]{:S(2)}) collective-permute-start(f32[16,1,2,64]{0,3,2,1:T(8,128)} %get-tuple-element.82), channel_id=1, source_target_pairs={{32,0},{64,32},{96,64},{128,96},{160,128},{192,160},{224,192},{33,... | collective-permute-start | bytes 24584 | tf_op jit(solution)/shard_map/ppermute | solution.py:22
  147.7 25.8 %collective-permute-start.13 = (f32[16,1,2,64]{0,3,2,1:T(8,128)}, f32[16,1,2,64]{0,3,2,1:T(8,128)S(1)}, u32[]{:S(2)}, u32[]{:S(2)}) collective-permute-start(f32[16,1,2,64]{0,3,2,1:T(8,128)} %get-tuple-element.81), channel_id=1, source_target_pairs={{0,32},{32,64},{64,96},{96,128},{128,160},{160,192},{192,224},{1,3... | collective-permute-start | bytes 24584 | tf_op jit(solution)/shard_map/ppermute | solution.py:21
  153.2 9.2 %collective-permute-start.18 = (f32[16,1,1,32]{0,3,1,2:T(8,128)S(1)}, f32[16,1,1,32]{0,3,1,2:T(8,128)S(1)}, u32[]{:S(2)}, u32[]{:S(2)}) collective-permute-start(f32[16,1,1,32]{0,3,1,2:T(8,128)S(1)} %get-tuple-element.110), channel_id=1, source_target_pairs={{32,0},{64,32},{96,64},{128,96},{160,128},{192,160},{224,192},{33,... | collective-permute-start | bytes 6152 | tf_op jit(solution)/shard_map/ppermute | solution.py:22
  154.5 11.9 %collective-permute-start.19 = (f32[16,1,1,32]{0,3,1,2:T(8,128)S(1)}, f32[16,1,1,32]{0,3,1,2:T(8,128)S(1)}, u32[]{:S(2)}, u32[]{:S(2)}) collective-permute-start(f32[16,1,1,32]{0,3,1,2:T(8,128)S(1)} %get-tuple-element.109), channel_id=1, source_target_pairs={{0,32},{32,64},{64,96},{96,128},{128,160},{160,192},{192,224},{1,3... | collective-permute-start | bytes 6152 | tf_op jit(solution)/shard_map/ppermute | solution.py:21
  160.9 49.8 %copy-start.44 = (f32[4,2,64]{2,1,0:T(2,128)}, f32[4,2,64]{2,1,0:T(2,128)S(1)}, u32[]{:S(2)}) copy-start(f32[4,2,64]{2,1,0:T(2,128)S(1)} %copy.668) | copy-start | bytes 6148
  161.1 31.8 %collective-permute-start.6 = (f32[16,1,4,128]{3,0,2,1:T(8,128)S(1)}, f32[16,1,4,128]{3,0,2,1:T(8,128)S(1)}, u32[]{:S(2)}, u32[]{:S(2)}) collective-permute-start(f32[16,1,4,128]{3,0,2,1:T(8,128)S(1)} %get-tuple-element.78), channel_id=1, source_target_pairs={{32,0},{64,32},{96,64},{128,96},{160,128},{192,160},{224,192},{33,... | collective-permute-start | bytes 98312 | tf_op jit(solution)/shard_map/ppermute | solution.py:22
  162.4 30.5 %collective-permute-start.7 = (f32[16,1,4,128]{3,0,2,1:T(8,128)S(1)}, f32[16,1,4,128]{3,0,2,1:T(8,128)S(1)}, u32[]{:S(2)}, u32[]{:S(2)}) collective-permute-start(f32[16,1,4,128]{3,0,2,1:T(8,128)S(1)} %get-tuple-element.77), channel_id=1, source_target_pairs={{0,32},{32,64},{64,96},{96,128},{128,160},{160,192},{192,224},{1,3... | collective-permute-start | bytes 98312 | tf_op jit(solution)/shard_map/ppermute | solution.py:21
  166.5 7.1 collective-permute-start.20
  170.8 4.0 collective-permute-start.21
  174.8 5.7 collective-permute-start.23
  176.9 7.8 collective-permute-start.22
  178.2 7.3 collective-permute-start.14
  180.5 5.4 collective-permute-start.15
  186.7 13.7 %collective-permute-start.16 = (f32[16,6,4,1]{3,0,2,1:T(8,128)}, f32[16,6,4,1]{3,0,2,1:T(8,128)S(1)}, u32[]{:S(2)}, u32[]{:S(2)}) collective-permute-start(f32[16,6,4,1]{3,0,2,1:T(8,128)} %get-tuple-element.93), channel_id=1, source_target_pairs={{1,0},{2,1},{3,2},{5,4},{6,5},{7,6},{9,8},{10,9},{11,10},{13,12},{... | collective-permute-start | bytes 4616 | tf_op jit(solution)/shard_map/ppermute | solution.py:22
  188.0 12.4 %collective-permute-start.17 = (f32[16,6,4,1]{3,0,2,1:T(8,128)}, f32[16,6,4,1]{3,0,2,1:T(8,128)S(1)}, u32[]{:S(2)}, u32[]{:S(2)}) collective-permute-start(f32[16,6,4,1]{3,0,2,1:T(8,128)} %get-tuple-element.94), channel_id=1, source_target_pairs={{0,1},{1,2},{2,3},{4,5},{5,6},{6,7},{8,9},{9,10},{10,11},{12,13},{... | collective-permute-start | bytes 4616 | tf_op jit(solution)/shard_map/ppermute | solution.py:21
  193.8 7.2 collective-permute-start.8
  195.7 6.3 collective-permute-start.9
  204.1 13.3 %collective-permute-start.11 = (f32[16,10,6,1]{3,0,2,1:T(8,128)}, f32[16,10,6,1]{3,0,2,1:T(8,128)}, u32[]{:S(2)}, u32[]{:S(2)}) collective-permute-start(f32[16,10,6,1]{3,0,2,1:T(8,128)} %get-tuple-element.50), channel_id=1, source_target_pairs={{0,1},{1,2},{2,3},{4,5},{5,6},{6,7},{8,9},{9,10},{10,11},{12,13},{... | collective-permute-start | bytes 11528 | tf_op jit(solution)/shard_map/ppermute | solution.py:21
  208.5 13.7 %collective-permute-start.10 = (f32[16,10,6,1]{3,0,2,1:T(8,128)}, f32[16,10,6,1]{3,0,2,1:T(8,128)}, u32[]{:S(2)}, u32[]{:S(2)}) collective-permute-start(f32[16,10,6,1]{3,0,2,1:T(8,128)} %get-tuple-element.49), channel_id=1, source_target_pairs={{1,0},{2,1},{3,2},{5,4},{6,5},{7,6},{9,8},{10,9},{11,10},{13,12},{... | collective-permute-start | bytes 11528 | tf_op jit(solution)/shard_map/ppermute | solution.py:22
  223.8 5.4 collective-permute-start.24
  225.1 5.2 collective-permute-start.25
  230.3 7.9 collective-permute-start.26
  232.6 6.9 collective-permute-start.27
  240.6 10.4 %collective-permute-start.29 = (f32[16,10,6,1]{3,0,2,1:T(8,128)}, f32[16,10,6,1]{3,0,2,1:T(8,128)}, u32[]{:S(2)}, u32[]{:S(2)}) collective-permute-start(f32[16,10,6,1]{3,0,2,1:T(8,128)} %get-tuple-element.46), channel_id=1, source_target_pairs={{0,1},{1,2},{2,3},{4,5},{5,6},{6,7},{8,9},{9,10},{10,11},{12,13},{... | collective-permute-start | bytes 11528 | tf_op jit(solution)/shard_map/ppermute | solution.py:21
  242.8 13.2 %collective-permute-start.28 = (f32[16,10,6,1]{3,0,2,1:T(8,128)}, f32[16,10,6,1]{3,0,2,1:T(8,128)}, u32[]{:S(2)}, u32[]{:S(2)}) collective-permute-start(f32[16,10,6,1]{3,0,2,1:T(8,128)} %get-tuple-element.45), channel_id=1, source_target_pairs={{1,0},{2,1},{3,2},{5,4},{6,5},{7,6},{9,8},{10,9},{11,10},{13,12},{... | collective-permute-start | bytes 11528 | tf_op jit(solution)/shard_map/ppermute | solution.py:22
  257.3 160.0 %copy-start.5 = (f32[16,8,4,128]{3,0,2,1:T(8,128)}, f32[16,8,4,128]{3,0,2,1:T(8,128)S(1)}, u32[]{:S(2)}) copy-start(f32[16,8,4,128]{3,0,2,1:T(8,128)S(1)} %fusion.68) | copy-start | bytes 786436
  546.1 26.4 %collective-permute-start.42 = (f32[16,1,2,64]{0,3,2,1:T(8,128)}, f32[16,1,2,64]{0,3,2,1:T(8,128)}, u32[]{:S(2)}, u32[]{:S(2)}) collective-permute-start(f32[16,1,2,64]{0,3,2,1:T(8,128)} %get-tuple-element.72), channel_id=1, source_target_pairs={{32,0},{64,32},{96,64},{128,96},{160,128},{192,160},{224,192},{33,... | collective-permute-start | bytes 24584 | tf_op jit(solution)/shard_map/ppermute | solution.py:22
  547.4 29.1 %collective-permute-start.43 = (f32[16,1,2,64]{0,3,2,1:T(8,128)}, f32[16,1,2,64]{0,3,2,1:T(8,128)}, u32[]{:S(2)}, u32[]{:S(2)}) collective-permute-start(f32[16,1,2,64]{0,3,2,1:T(8,128)} %get-tuple-element.71), channel_id=1, source_target_pairs={{0,32},{32,64},{64,96},{96,128},{128,160},{160,192},{192,224},{1,3... | collective-permute-start | bytes 24584 | tf_op jit(solution)/shard_map/ppermute | solution.py:21
  553.0 11.1 %collective-permute-start.48 = (f32[16,1,1,32]{0,3,1,2:T(8,128)S(1)}, f32[16,1,1,32]{0,3,1,2:T(8,128)S(1)}, u32[]{:S(2)}, u32[]{:S(2)}) collective-permute-start(f32[16,1,1,32]{0,3,1,2:T(8,128)S(1)} %get-tuple-element.108), channel_id=1, source_target_pairs={{32,0},{64,32},{96,64},{128,96},{160,128},{192,160},{224,192},{33,... | collective-permute-start | bytes 6152 | tf_op jit(solution)/shard_map/ppermute | solution.py:22
  554.4 13.8 %collective-permute-start.49 = (f32[16,1,1,32]{0,3,1,2:T(8,128)S(1)}, f32[16,1,1,32]{0,3,1,2:T(8,128)S(1)}, u32[]{:S(2)}, u32[]{:S(2)}) collective-permute-start(f32[16,1,1,32]{0,3,1,2:T(8,128)S(1)} %get-tuple-element.107), channel_id=1, source_target_pairs={{0,32},{32,64},{64,96},{96,128},{128,160},{160,192},{192,224},{1,3... | collective-permute-start | bytes 6152 | tf_op jit(solution)/shard_map/ppermute | solution.py:21
  562.0 25.6 %collective-permute-start.36 = (f32[16,1,4,128]{3,0,2,1:T(8,128)S(1)}, f32[16,1,4,128]{3,0,2,1:T(8,128)S(1)}, u32[]{:S(2)}, u32[]{:S(2)}) collective-permute-start(f32[16,1,4,128]{3,0,2,1:T(8,128)S(1)} %get-tuple-element.70), channel_id=1, source_target_pairs={{32,0},{64,32},{96,64},{128,96},{160,128},{192,160},{224,192},{33,... | collective-permute-start | bytes 98312 | tf_op jit(solution)/shard_map/ppermute | solution.py:22
  564.2 23.5 %collective-permute-start.37 = (f32[16,1,4,128]{3,0,2,1:T(8,128)S(1)}, f32[16,1,4,128]{3,0,2,1:T(8,128)S(1)}, u32[]{:S(2)}, u32[]{:S(2)}) collective-permute-start(f32[16,1,4,128]{3,0,2,1:T(8,128)S(1)} %get-tuple-element.69), channel_id=1, source_target_pairs={{0,32},{32,64},{64,96},{96,128},{128,160},{160,192},{192,224},{1,3... | collective-permute-start | bytes 98312 | tf_op jit(solution)/shard_map/ppermute | solution.py:21
  568.2 9.2 %collective-permute-start.50 = (f32[16,4,1,32]{0,3,1,2:T(8,128)S(1)}, f32[16,4,1,32]{0,3,1,2:T(8,128)S(1)}, u32[]{:S(2)}, u32[]{:S(2)}) collective-permute-start(f32[16,4,1,32]{0,3,1,2:T(8,128)S(1)} %pad_maximum_fusion.177), channel_id=1, source_target_pairs={{4,0},{8,4},{12,8},{16,12},{20,16},{24,20},{28,24},{5,1},{9,5},{13... | collective-permute-start | bytes 24584 | tf_op jit(solution)/shard_map/ppermute | solution.py:22
  572.4 4.9 collective-permute-start.51
  577.4 6.1 collective-permute-start.53
  579.5 7.3 collective-permute-start.52
  580.8 13.0 %collective-permute-start.44 = (f32[16,6,1,64]{3,0,2,1:T(8,128)S(1)}, f32[16,6,1,64]{3,0,2,1:T(8,128)S(1)}, u32[]{:S(2)}, u32[]{:S(2)}) collective-permute-start(f32[16,6,1,64]{3,0,2,1:T(8,128)S(1)} %get-tuple-element.98), channel_id=1, source_target_pairs={{4,0},{8,4},{12,8},{16,12},{20,16},{24,20},{28,24},{5,1},{9,5},{13... | collective-permute-start | bytes 73736 | tf_op jit(solution)/shard_map/ppermute | solution.py:22
  583.5 10.3 %collective-permute-start.45 = (f32[16,6,1,64]{3,0,2,1:T(8,128)S(1)}, f32[16,6,1,64]{3,0,2,1:T(8,128)S(1)}, u32[]{:S(2)}, u32[]{:S(2)}) collective-permute-start(f32[16,6,1,64]{3,0,2,1:T(8,128)S(1)} %get-tuple-element.97), channel_id=1, source_target_pairs={{0,4},{4,8},{8,12},{12,16},{16,20},{20,24},{24,28},{1,5},{5,9},{9,... | collective-permute-start | bytes 73736 | tf_op jit(solution)/shard_map/ppermute | solution.py:21
  588.3 17.2 %collective-permute-start.38 = (f32[16,10,1,128]{3,0,2,1:T(8,128)}, f32[16,10,1,128]{3,0,2,1:T(8,128)}, u32[]{:S(2)}, u32[]{:S(2)}) collective-permute-start(f32[16,10,1,128]{3,0,2,1:T(8,128)} %get-tuple-element.56), channel_id=1, source_target_pairs={{4,0},{8,4},{12,8},{16,12},{20,16},{24,20},{28,24},{5,1},{9,5},{13... | collective-permute-start | bytes 245768 | tf_op jit(solution)/shard_map/ppermute | solution.py:22
  590.2 15.3 %collective-permute-start.39 = (f32[16,10,1,128]{3,0,2,1:T(8,128)}, f32[16,10,1,128]{3,0,2,1:T(8,128)}, u32[]{:S(2)}, u32[]{:S(2)}) collective-permute-start(f32[16,10,1,128]{3,0,2,1:T(8,128)} %get-tuple-element.55), channel_id=1, source_target_pairs={{0,4},{4,8},{8,12},{12,16},{16,20},{20,24},{24,28},{1,5},{5,9},{9,... | collective-permute-start | bytes 245768 | tf_op jit(solution)/shard_map/ppermute | solution.py:21
  594.0 9.0 %collective-permute-start.46 = (f32[16,6,4,1]{3,0,2,1:T(8,128)S(1)}, f32[16,6,4,1]{3,0,2,1:T(8,128)S(1)}, u32[]{:S(2)}, u32[]{:S(2)}) collective-permute-start(f32[16,6,4,1]{3,0,2,1:T(8,128)S(1)} %get-tuple-element.87), channel_id=1, source_target_pairs={{1,0},{2,1},{3,2},{5,4},{6,5},{7,6},{9,8},{10,9},{11,10},{13,12},{... | collective-permute-start | bytes 4616 | tf_op jit(solution)/shard_map/ppermute | solution.py:22
  595.3 9.5 %collective-permute-start.47 = (f32[16,6,4,1]{3,0,2,1:T(8,128)S(1)}, f32[16,6,4,1]{3,0,2,1:T(8,128)S(1)}, u32[]{:S(2)}, u32[]{:S(2)}) collective-permute-start(f32[16,6,4,1]{3,0,2,1:T(8,128)S(1)} %get-tuple-element.88), channel_id=1, source_target_pairs={{0,1},{1,2},{2,3},{4,5},{5,6},{6,7},{8,9},{9,10},{10,11},{12,13},{... | collective-permute-start | bytes 4616 | tf_op jit(solution)/shard_map/ppermute | solution.py:21
  607.6 14.4 %collective-permute-start.41 = (f32[16,10,6,1]{3,0,2,1:T(8,128)}, f32[16,10,6,1]{3,0,2,1:T(8,128)}, u32[]{:S(2)}, u32[]{:S(2)}) collective-permute-start(f32[16,10,6,1]{3,0,2,1:T(8,128)} %get-tuple-element.44), channel_id=1, source_target_pairs={{0,1},{1,2},{2,3},{4,5},{5,6},{6,7},{8,9},{9,10},{10,11},{12,13},{... | collective-permute-start | bytes 11528 | tf_op jit(solution)/shard_map/ppermute | solution.py:21
  612.3 14.3 %collective-permute-start.40 = (f32[16,10,6,1]{3,0,2,1:T(8,128)}, f32[16,10,6,1]{3,0,2,1:T(8,128)}, u32[]{:S(2)}, u32[]{:S(2)}) collective-permute-start(f32[16,10,6,1]{3,0,2,1:T(8,128)} %get-tuple-element.43), channel_id=1, source_target_pairs={{1,0},{2,1},{3,2},{5,4},{6,5},{7,6},{9,8},{10,9},{11,10},{13,12},{... | collective-permute-start | bytes 11528 | tf_op jit(solution)/shard_map/ppermute | solution.py:22
  628.6 5.4 collective-permute-start.54
  629.9 5.0 collective-permute-start.55
  635.0 7.3 collective-permute-start.56
  639.7 3.9 collective-permute-start.57
  644.7 14.0 %collective-permute-start.59 = (f32[16,10,6,1]{3,0,2,1:T(8,128)}, f32[16,10,6,1]{3,0,2,1:T(8,128)}, u32[]{:S(2)}, u32[]{:S(2)}) collective-permute-start(f32[16,10,6,1]{3,0,2,1:T(8,128)} %get-tuple-element.42), channel_id=1, source_target_pairs={{0,1},{1,2},{2,3},{4,5},{5,6},{6,7},{8,9},{9,10},{10,11},{12,13},{... | collective-permute-start | bytes 11528 | tf_op jit(solution)/shard_map/ppermute | solution.py:21
  648.6 15.2 %collective-permute-start.58 = (f32[16,10,6,1]{3,0,2,1:T(8,128)}, f32[16,10,6,1]{3,0,2,1:T(8,128)}, u32[]{:S(2)}, u32[]{:S(2)}) collective-permute-start(f32[16,10,6,1]{3,0,2,1:T(8,128)} %get-tuple-element.41), channel_id=1, source_target_pairs={{1,0},{2,1},{3,2},{5,4},{6,5},{7,6},{9,8},{10,9},{11,10},{13,12},{... | collective-permute-start | bytes 11528 | tf_op jit(solution)/shard_map/ppermute | solution.py:22
  (63 other events, 1042.7 us)
